TPU v7x, 512 devices: a whole 4x8x8 slice. The times are simulated.
512 devices in a mesh: lon: 64 (over y_hi, x, z), mlp: 8 (over y_lo, core).
Axes of the slice: x: 4, y: 8 (y_hi: 2, y_lo: 4; y = y_hi * 4 + y_lo), z: 8, core: 2. Of those that a mesh axis runs over, the one named last changes fastest.
Arguments:
- fields: bfloat16 [48, 1472, 1024], P('mlp', 'lon'), may hold values from -40 to 40
- cotangent: bfloat16 [48, 1472, 1024], P('mlp', 'lon'), may hold values from -6 to 6
- conv_weight: bfloat16 [7, 7, 1024], replicated, may hold values from -0.875 to 0.875
- norm_gain: bfloat16 [1024], replicated, may hold values from 0.099609375 to 1.8984375
- weight_in: bfloat16 [1024, 4096], P(None, 'mlp'), may hold values from -0.1875 to 0.1875
- weight_out: bfloat16 [4096, 1024], P('mlp'), may hold values from -0.09375 to 0.09375
Outputs:
- grad_fields: bfloat16 [48, 1472, 1024], P('mlp', 'lon')
- grad_weight_in: bfloat16 [1024, 4096], P(None, 'mlp')
- grad_weight_out: bfloat16 [4096, 1024], P('mlp')
All inputs are finite; a program needn't handle non-finite values.
Results may differ from a plain program's by a relative error of at most 0.0095.
Values may be sent and summed in bfloat16 or wider, within the bound.
A program may use at most 64 MiB of HBM per device.

v0:
```python
import math

import jax
import jax.numpy as jnp
from jax import lax
from jax.sharding import PartitionSpec as P

KS = 7
LON = 1440


def passed_along(value, axis, by):
    count = lax.axis_size(axis)
    return lax.ppermute(value, axis, [(i, (i + by) % count) for i in range(count)])


def with_halo(cells, sides, width):
    for axis, dim in sides:
        count = lax.axis_size(axis)
        ends = count - 1
        head = lax.slice_in_dim(cells, 0, width, axis=dim)
        tail = lax.slice_in_dim(cells, cells.shape[dim] - width, cells.shape[dim], axis=dim)
        cells = jnp.concatenate(
            [
                lax.ppermute(tail, axis, [(i, (i + 1) % count) for i in range(ends)]),
                cells,
                lax.ppermute(head, axis, [((i + 1) % count, i) for i in range(ends)]),
            ],
            axis=dim,
        )
    return cells


def activate(values):
    return values * (0.5 * (1.0 + lax.erf(values * (1.0 / math.sqrt(2.0)))))


def slope(values):
    cumulative = 0.5 * (1.0 + lax.erf(values * (1.0 / math.sqrt(2.0))))
    return cumulative + values * jnp.exp(-0.5 * values * values) * (1.0 / math.sqrt(2.0 * math.pi))


def live_count():
    members = lax.axis_size("lon")
    position = lax.axis_index("lon")
    return LON // members + (position < LON % members).astype(jnp.int32)


def lon_cycle(field, held):
    reach = KS // 2
    first_cols = field[:, :reach]
    last_cols = lax.dynamic_slice_in_dim(field, held - reach, reach, 1)
    from_left = passed_along(last_cols, "lon", 1)
    from_right = passed_along(first_cols, "lon", -1)
    spare = jnp.zeros((field.shape[0], reach, field.shape[2]), field.dtype)
    joined = jnp.concatenate([from_left, field, spare], axis=1)
    return lax.dynamic_update_slice_in_dim(joined, from_right, reach + held, 1)


def extend(field, held):
    reach = KS // 2
    rows = with_halo(field, (("mlp", 0),), reach)
    padded = lon_cycle(rows, held)
    return padded.astype(jnp.float32)


def body(fields, cotangent, conv_weight, norm_gain, weight_in, weight_out):
    lat_dev, slot_count, width = fields.shape
    reach = KS // 2
    held = live_count()
    slot_live = lax.broadcasted_iota(jnp.int32, (1, slot_count, 1), 1) < held
    kernel = conv_weight.astype(jnp.float32)
    padded = extend(fields, held)
    mixed = jnp.zeros((lat_dev, slot_count, width), jnp.float32)
    for row_off in range(KS):
        for col_off in range(KS):
            mixed = (
                mixed
                + kernel[row_off, col_off]
                * padded[row_off : row_off + lat_dev, col_off : col_off + slot_count]
            )
    centred = mixed - jnp.mean(mixed, axis=-1, keepdims=True)
    inv_std = lax.rsqrt(jnp.mean(centred * centred, axis=-1, keepdims=True) + 1e-06)
    norm_hat = centred * inv_std
    gain = norm_gain.astype(jnp.float32)
    normed = jnp.where(slot_live, norm_hat * gain, 0.0).astype(jnp.bfloat16).reshape(-1, width)
    normed_all = lax.all_gather(normed, "mlp", axis=0, tiled=True)
    cot_all = lax.all_gather(cotangent.reshape(-1, width), "mlp", axis=0, tiled=True)
    hidden = jnp.dot(normed_all, weight_in, preferred_element_type=jnp.float32)
    activated = activate(hidden).astype(jnp.bfloat16)
    upstream = lax.dot_general(
        cot_all, weight_out, (((1,), (1,)), ((), ())), preferred_element_type=jnp.float32
    )
    grad_hidden = (upstream * slope(hidden)).astype(jnp.bfloat16)
    grad_second = lax.dot_general(
        activated, cot_all, (((0,), (0,)), ((), ())), preferred_element_type=jnp.float32
    )
    grad_first = lax.dot_general(
        normed_all, grad_hidden, (((0,), (0,)), ((), ())), preferred_element_type=jnp.float32
    )
    grad_normed = lax.psum_scatter(
        lax.dot_general(
            grad_hidden, weight_in, (((1,), (1,)), ((), ())), preferred_element_type=jnp.float32
        ).astype(jnp.bfloat16),
        "mlp",
        scatter_dimension=0,
        tiled=True,
    ).astype(jnp.float32)
    cells = lax.axis_size("mlp") * lat_dev * LON
    factor = jnp.float32(1.0 / math.sqrt(cells))
    summed_first, summed_second = lax.psum((grad_first, grad_second), "lon")
    out_first = (summed_first * factor).astype(jnp.bfloat16)
    out_second = (summed_second * factor).astype(jnp.bfloat16)
    scaled = grad_normed.reshape(lat_dev, slot_count, width) * gain
    grad_mixed = inv_std * (
        scaled
        - jnp.mean(scaled, axis=-1, keepdims=True)
        - norm_hat * jnp.mean(scaled * norm_hat, axis=-1, keepdims=True)
    )
    grad_mixed = grad_mixed.astype(jnp.bfloat16)
    padded_grad = extend(grad_mixed, held)
    result = cotangent.astype(jnp.float32)
    for row_off in range(KS):
        for col_off in range(KS):
            row_start = 2 * reach - row_off
            col_start = 2 * reach - col_off
            result = (
                result
                + kernel[row_off, col_off]
                * padded_grad[row_start : row_start + lat_dev, col_start : col_start + slot_count]
            )
    result = jnp.where(slot_live, result, 0.0)
    return (result.astype(jnp.bfloat16), out_first, out_second)


def solution(mesh):
    in_specs = (
        P("mlp", "lon", None),
        P("mlp", "lon", None),
        P(),
        P(),
        P(None, "mlp"),
        P("mlp", None),
    )
    out_specs = (P("mlp", "lon", None), P(None, "mlp"), P("mlp", None))
    return jax.shard_map(body, mesh=mesh, in_specs=in_specs, out_specs=out_specs, check_vma=False)
```

profile of v0, /device:TPU:56, one launch (start us, length us, event | category | flops | bytes accessed | tf_op | source)
XLA Modules:
  0.0 991.0 jit_solution(17638679118081146668)
XLA Ops:
  7.2 1.9 reshape.50
  10.2 1.9 collective-permute-start
  12.1 3.6 collective-permute-start.1
  20.2 4.3 collective-permute-start.2
  24.5 13.0 %collective-permute-start.3 = (bf16[12,3,1024]{2,1,0:T(4,128)(2,1)S(1)}, bf16[12,3,1024]{2,1,0:T(4,128)(2,1)S(1)}, u32[]{:S(2)}, u32[]{:S(2)}) collective-permute-start(bf16[12,3,1024]{2,1,0:T(4,128)(2,1)S(1)} %get-tuple-element.9), channel_id=1, source_target_pairs={{0,504},{8,0},{16,8},{24,16},{32,24},{40,32},{48,40},{56,48},{64,5... | collective-permute-start | bytes 221192 | tf_op jit(solution)/shard_map/ppermute | solution.py:14
  37.5 3.0 collective-permute-done.2
  40.9 1.5 collective-permute-done.3
  42.4 1.3 dynamic_update_slice.6
  43.9 6.2 fusion.106
  51.4 6.6 all-gather.5.cloned.1.call-done
  58.0 3.0 reshape.51
  61.0 39.1 %all-gather.7.cloned.1.call-done = bf16[8,138,1024]{2,1,0:T(8,128)(2,1)} async-done(((bf16[1,138,1024]{2,1,0:T(8,128)(2,1)}), bf16[8,138,1024]{2,1,0:T(8,128)(2,1)}) %all-gather.7.cloned.1.call-update) | async-done | bytes 2261008 | tf_op jit(solution)/shard_map/all_gather | solution.py:87
  100.1 2.9 reshape.53
  103.0 3.1 fusion.115
  106.2 2.9 fusion.6
  109.1 2.0 fusion.1
  112.2 2.9 fusion.116
  115.1 4.1 convolution_convert_fusion
  119.2 33.0 %fusion = bf16[144,1024]{1,0:T(8,128)(2,1)S(1)} fusion(bf16[1104,1024]{1,0:T(8,128)(2,1)} %convolution_convert_fusion), kind=kCustom, calls=%all-reduce-scatter | all-reduce-scatter fusion | flops 1179649 | bytes 2557952
  152.2 2.8 collective-permute-start.8
  155.1 1.3 dynamic-slice.4
  159.6 1.9 collective-permute-start.4
  161.5 3.6 collective-permute-start.5
  165.2 1.3 collective-permute-done.4
  166.5 1.8 collective-permute-done.5
  168.5 1.9 collective-permute-start.6
  170.4 12.0 %collective-permute-start.7 = (bf16[12,3,1024]{2,1,0:T(4,128)(2,1)S(1)}, bf16[12,3,1024]{2,1,0:T(4,128)(2,1)S(1)}, u32[]{:S(2)}, u32[]{:S(2)}) collective-permute-start(bf16[12,3,1024]{2,1,0:T(4,128)(2,1)S(1)} %get-tuple-element.7), channel_id=1, source_target_pairs={{0,504},{8,0},{16,8},{24,16},{32,24},{40,32},{48,40},{56,48},{64,5... | collective-permute-start | bytes 221192 | tf_op jit(solution)/shard_map/ppermute | solution.py:14
  182.5 2.3 collective-permute-done.6
  186.1 1.3 dynamic_update_slice.7
  187.7 4.9 fusion.9
  192.6 787.7 %all-reduce.5.cloned.1.call-done = (f32[1024,512]{1,0:T(8,128)}, f32[512,1024]{1,0:T(8,128)}) async-done(((f32[1024,512]{1,0:T(8,128)}, f32[512,1024]{1,0:T(8,128)}), (f32[1024,512]{1,0:T(8,128)}, f32[512,1024]{1,0:T(8,128)})) %all-reduce.5.cloned.1.call-update) | async-done | bytes 4194320 | tf_op jit(solution)/shard_map/psum | solution.py:111
  980.3 3.0 multiply_convert_fusion.1
  (61 shorter events, 13.8 us)
Async XLA Ops:
  7.2 95.8 %copy-start = (bf16[1024,512]{1,0:T(8,128)(2,1)S(1)}, bf16[1024,512]{1,0:T(8,128)(2,1)}, u32[]{:S(2)}) copy-start(bf16[1024,512]{1,0:T(8,128)(2,1)} %param.10) | copy-start | bytes 3145732
  7.2 12.8 %copy-start.4 = (bf16[6,23,1024]{2,1,0:T(8,128)(2,1)S(1)}, bf16[6,23,1024]{2,1,0:T(8,128)(2,1)}, u32[]{:S(2)}) copy-start(bf16[6,23,1024]{2,1,0:T(8,128)(2,1)} %param.6) | copy-start | bytes 847876
  7.2 50.8 %all-gather.5.cloned.1.call-start = ((), (), s32[]{:S(2)}) async-start(), calls=%async_computation | async-start | bytes 2654208 | tf_op jit(solution)/shard_map/all_gather | solution.py:88
  9.1 90.9 %all-gather.7.cloned.1.call-start = ((), (), s32[]{:S(2)}) async-start(), calls=%async_computation.1 | async-start | bytes 2654208 | tf_op jit(solution)/shard_map/all_gather | solution.py:87
  10.2 9.8 collective-permute-start
  12.1 7.9 collective-permute-start.1
  20.2 20.4 %collective-permute-start.2 = (bf16[12,3,1024]{2,1,0:T(4,128)(2,1)S(1)}, bf16[12,3,1024]{2,1,0:T(4,128)(2,1)S(1)}, u32[]{:S(2)}, u32[]{:S(2)}) collective-permute-start(bf16[12,3,1024]{2,1,0:T(4,128)(2,1)S(1)} %get-tuple-element.10), channel_id=1, source_target_pairs={{0,8},{8,16},{16,24},{24,32},{32,40},{40,48},{48,56},{56,64},{64,7... | collective-permute-start | bytes 221192 | tf_op jit(solution)/shard_map/ppermute | solution.py:14
  24.5 17.8 %collective-permute-start.3 = (bf16[12,3,1024]{2,1,0:T(4,128)(2,1)S(1)}, bf16[12,3,1024]{2,1,0:T(4,128)(2,1)S(1)}, u32[]{:S(2)}, u32[]{:S(2)}) collective-permute-start(bf16[12,3,1024]{2,1,0:T(4,128)(2,1)S(1)} %get-tuple-element.9), channel_id=1, source_target_pairs={{0,504},{8,0},{16,8},{24,16},{32,24},{40,32},{48,40},{56,48},{64,5... | collective-permute-start | bytes 221192 | tf_op jit(solution)/shard_map/ppermute | solution.py:14
  51.3 928.9 %all-reduce.5.cloned.1.call-start = ((), (), s32[]{:S(2)}) async-start(), calls=%async_computation.2 | async-start | bytes 8388608 | tf_op jit(solution)/shard_map/psum | solution.py:111
  103.0 3.1 copy-start.1
  106.2 2.9 copy-start.6
  109.1 3.1 copy-start.2
  111.1 1.1 copy-start.7
  152.2 5.9 collective-permute-start.8
  159.6 6.9 collective-permute-start.4
  161.5 6.8 collective-permute-start.5
  168.4 19.3 %copy-start.5 = (bf16[6,23,1024]{2,1,0:T(8,128)(2,1)S(1)}, bf16[6,23,1024]{2,1,0:T(8,128)(2,1)}, u32[]{:S(2)}) copy-start(bf16[6,23,1024]{2,1,0:T(8,128)(2,1)} %param.7) | copy-start | bytes 847876
  168.5 16.3 %collective-permute-start.6 = (bf16[12,3,1024]{2,1,0:T(4,128)(2,1)S(1)}, bf16[12,3,1024]{2,1,0:T(4,128)(2,1)S(1)}, u32[]{:S(2)}, u32[]{:S(2)}) collective-permute-start(bf16[12,3,1024]{2,1,0:T(4,128)(2,1)S(1)} %get-tuple-element.8), channel_id=1, source_target_pairs={{0,8},{8,16},{16,24},{24,32},{32,40},{40,48},{48,56},{56,64},{64,7... | collective-permute-start | bytes 221192 | tf_op jit(solution)/shard_map/ppermute | solution.py:14
  170.4 15.7 %collective-permute-start.7 = (bf16[12,3,1024]{2,1,0:T(4,128)(2,1)S(1)}, bf16[12,3,1024]{2,1,0:T(4,128)(2,1)S(1)}, u32[]{:S(2)}, u32[]{:S(2)}) collective-permute-start(bf16[12,3,1024]{2,1,0:T(4,128)(2,1)S(1)} %get-tuple-element.7), channel_id=1, source_target_pairs={{0,504},{8,0},{16,8},{24,16},{32,24},{40,32},{48,40},{56,48},{64,5... | collective-permute-start | bytes 221192 | tf_op jit(solution)/shard_map/ppermute | solution.py:14
  980.3 3.0 copy-start.3
Sparse Core Ops, SparseCore 0:
  10.7 47.2 all-gather.4
  60.6 39.4 all-gather.6
  119.3 860.9 all-reduce.4
where the time goes:
time: 993 us; the launch traced here: 991 us
  waiting for transfers between devices  846 us (85%)
  starting transfers between devices  45.4 us (5%)
  blocking collectives  33 us (3%)
  local copies, waits for them, and re-layouts  19.1 us (2%)
  other arithmetic  18.2 us (2%)
  matrix products  15 us (2%)
  between operations  14.8 us (1%)
    psum x1, waiting for transfers between devices, body(): summed_first, summed_second = lax.psum((grad_first, grad_second), 'lon')  788 us
    all_gather x1, waiting for transfers between devices, body(): normed_all = lax.all_gather(normed, 'mlp', axis=0, tiled=True)  39.1 us
    unnamed x1, blocking collectives  33 us
    ppermute x4, starting transfers between devices, passed_along(): lax.ppermute(value, axis, [(i, (i + by) % count) for i in range(count)])  31.3 us
  transfers between devices with their start and end apart: 12, of which 10 were waited for; matrix products, arithmetic and copies ran while one was open for 6% of the time, Pallas kernels for 0%

commit v1 on v0

--- a/solution.py
+++ b/solution.py
@@ -3,10 +3,212 @@
 import jax
 import jax.numpy as jnp
 from jax import lax
+from jax.experimental import pallas as pl
+from jax.experimental.pallas import tpu as pltpu
 from jax.sharding import PartitionSpec as P
 
 KS = 7
 LON = 1440
+
+
+N_Z, N_X, N_YH = 8, 4, 2
+MESH = pl.DeviceIdType.MESH
+BF = jnp.bfloat16
+F32 = jnp.float32
+
+
+class Sends:
+    def __init__(self, send_sems, recv_sems):
+        self.send_sems, self.recv_sems, self.started = send_sems, recv_sems, []
+
+    def start(self, src, dst, device):
+        index = len(self.started)
+        copy = pltpu.make_async_remote_copy(
+            src_ref=src,
+            dst_ref=dst,
+            send_sem=self.send_sems.at[index],
+            recv_sem=self.recv_sems.at[index],
+            device_id=device,
+            device_id_type=MESH,
+        )
+        copy.start()
+        self.started.append(copy)
+        return copy
+
+    def finish(self):
+        for copy in self.started:
+            copy.wait_send()
+
+
+def block(ref, start, size):
+    return ref.at[pl.ds(pl.multiple_of(start, size), size)]
+
+
+def ring_reduce(sends, own, stage, recv, me, count, at):
+    half = stage.shape[3]
+    arrived = {}
+    levels = count // 2
+    for slot in range(levels):
+        for late in (0, 1):
+            level = levels - slot - late
+            if level < 1:
+                continue
+            for way in (0, 1):
+                sub = way if late == 0 else 1 - way
+                step = 1 if way == 0 else -1
+                target = lax.rem(me + step * level + count, count)
+                value = block(own, target * (2 * half) + sub * half, half)[...]
+                before = arrived.get((level + 1, way, sub))
+                if before is not None:
+                    before.wait_recv()
+                    value = value + recv[level, way, sub].astype(F32)
+                stage[level - 1, way, sub] = value.astype(BF)
+                arrived[level, way, sub] = sends.start(
+                    stage.at[level - 1, way, sub],
+                    recv.at[level - 1, way, sub],
+                    at(lax.rem(me + step + count, count)),
+                )
+        yield
+    for way in (0, 1):
+        for sub in (0, 1):
+            arrived[1, way, sub].wait_recv()
+
+
+def ring_gather(sends, out, me, count, at, half):
+    arrived = {}
+    levels = count // 2
+    for level in range(levels):
+        for sub in (0, 1):
+            for way in (0, 1):
+                if level == levels - 1 and sub != way:
+                    continue
+                step = 1 if way == 0 else -1
+                if level > 0:
+                    arrived[level - 1, way, sub].wait_recv()
+                chunk = lax.rem(me - step * level + count, count)
+                rows = block(out, chunk * (2 * half) + sub * half, half)
+                arrived[level, way, sub] = sends.start(
+                    rows, rows, at(lax.rem(me + step + count, count))
+                )
+        yield
+    for way in (0, 1):
+        for sub in (0, 1):
+            last = levels - 1 if sub == way else levels - 2
+            if last >= 0:
+                arrived[last, way, sub].wait_recv()
+
+
+def ring_sum(own, recv, me, half):
+    for sub in (0, 1):
+        value = block(own, me * (2 * half) + sub * half, half)[...]
+        yield sub, value + recv[0, 0, sub].astype(F32) + recv[0, 1, sub].astype(F32)
+
+
+def reduce_all(sends, own, out, bufs, ring, line, far, factor):
+    stage, recv, flat, pieces, mine, theirs = bufs
+    (ring_me, ring_count, ring_at), (line_me, line_count, line_at) = ring, line
+    half = stage.shape[3]
+    piece = mine.shape[0]
+    yield from ring_reduce(sends, own, stage, recv, ring_me, ring_count, ring_at)
+    for sub, value in ring_sum(own, recv, ring_me, half):
+        flat[pl.ds(sub * half, half)] = value.astype(BF)
+    copies = []
+    for offset in range(1, line_count):
+        target = lax.rem(line_me + offset, line_count)
+        copies.append(
+            sends.start(block(flat, target * piece, piece), pieces.at[offset - 1], line_at(target))
+        )
+    yield
+    total = block(flat, line_me * piece, piece)[...].astype(F32)
+    for offset, copy in enumerate(copies):
+        copy.wait_recv()
+        total = total + pieces[offset].astype(F32)
+    mine[...] = total.astype(BF)
+    copy = sends.start(mine, theirs, far)
+    yield
+    copy.wait_recv()
+    total = (mine[...].astype(F32) + theirs[...].astype(F32)) * factor
+    place = block(out, ring_me * (2 * half) + line_me * piece, piece)
+    place[...] = total.astype(BF)
+    copies = []
+    for offset in range(1, line_count):
+        target = lax.rem(line_me + offset, line_count)
+        copies.append(sends.start(place, place, line_at(target)))
+    yield
+    for copy in copies:
+        copy.wait_recv()
+    yield from ring_gather(sends, out, ring_me, ring_count, ring_at, half)
+
+
+def interleave(*parts):
+    live = list(parts)
+    while live:
+        live = [part for part in live if next(part, StopIteration) is not StopIteration]
+
+
+def reduce_buffers(levels, half, width, line_count):
+    piece = 2 * half // line_count
+    return [
+        pltpu.VMEM((levels, 2, 2, half, width), BF),
+        pltpu.VMEM((levels, 2, 2, half, width), BF),
+        pltpu.VMEM((2 * half, width), BF),
+        pltpu.VMEM((line_count - 1, piece, width), BF),
+        pltpu.VMEM((piece, width), BF),
+        pltpu.VMEM((piece, width), BF),
+    ]
+
+
+def reduce_kernel(factor, first, second, out_first, out_second, *scratch):
+    bufs_first, bufs_second, (send_sems, recv_sems) = scratch[:6], scratch[6:12], scratch[12:]
+    lon, mlp = lax.axis_index("lon"), lax.axis_index("mlp")
+    z = lax.rem(lon, N_Z)
+    x = lax.rem(lax.div(lon, N_Z), N_X)
+    high = lax.div(lon, N_X * N_Z)
+
+    def place(far, along_x, along_z):
+        return (far * (N_X * N_Z) + along_x * N_Z + along_z, mlp)
+
+    def at_x(other):
+        return place(high, other, z)
+
+    def at_z(other):
+        return place(high, x, other)
+
+    far = place(1 - high, x, z)
+    barrier = pltpu.get_barrier_semaphore()
+    peers = [at_z(lax.rem(z + k, N_Z)) for k in range(1, N_Z)]
+    peers += [at_x(lax.rem(x + k, N_X)) for k in range(1, N_X)]
+    peers.append(far)
+    for peer in peers:
+        pl.semaphore_signal(barrier, inc=1, device_id=peer, device_id_type=MESH)
+    pl.semaphore_wait(barrier, len(peers))
+    sends = Sends(send_sems, recv_sems)
+    along_x, along_z = (x, N_X, at_x), (z, N_Z, at_z)
+    interleave(
+        reduce_all(sends, first, out_first, bufs_first, along_z, along_x, far, factor),
+        reduce_all(sends, second, out_second, bufs_second, along_x, along_z, far, factor),
+    )
+    sends.finish()
+
+
+def reduce_weights(first, second, factor):
+    vmem = pl.BlockSpec(memory_space=pltpu.VMEM)
+    return pl.pallas_call(
+        lambda *refs: reduce_kernel(factor, *refs),
+        out_shape=(
+            jax.ShapeDtypeStruct(first.shape, BF),
+            jax.ShapeDtypeStruct(second.shape, BF),
+        ),
+        in_specs=[vmem, vmem],
+        out_specs=(vmem, vmem),
+        scratch_shapes=reduce_buffers(N_Z // 2, 64, first.shape[1], N_X)
+        + reduce_buffers(N_X // 2, 64, second.shape[1], N_Z)
+        + [pltpu.SemaphoreType.DMA((96,)), pltpu.SemaphoreType.DMA((96,))],
+        compiler_params=pltpu.CompilerParams(
+            collective_id=0, has_side_effects=True, vmem_limit_bytes=40 << 20
+        ),
+        name="reduce_weights",
+    )(first, second)
 
 
 def passed_along(value, axis, by):
@@ -107,10 +309,7 @@
         tiled=True,
     ).astype(jnp.float32)
     cells = lax.axis_size("mlp") * lat_dev * LON
-    factor = jnp.float32(1.0 / math.sqrt(cells))
-    summed_first, summed_second = lax.psum((grad_first, grad_second), "lon")
-    out_first = (summed_first * factor).astype(jnp.bfloat16)
-    out_second = (summed_second * factor).astype(jnp.bfloat16)
+    out_first, out_second = reduce_weights(grad_first, grad_second, 1.0 / math.sqrt(cells))
     scaled = grad_normed.reshape(lat_dev, slot_count, width) * gain
     grad_mixed = inv_std * (
         scaled

time: 993 us -> 262 us (0.26)
  the two profiles are of different devices: /device:TPU:56 before, /device:TPU:16 now
where the time goes in v1:
time: 262 us; the launch traced here: 261 us
  Pallas kernels  69.2 us (26%)
  starting transfers between devices  44.3 us (17%)
  waiting for transfers between devices  43.9 us (17%)
  blocking collectives  29.7 us (11%)
  local copies, waits for them, and re-layouts  23.9 us (9%)
  other arithmetic  19.9 us (8%)
  between operations  16.4 us (6%)
  matrix products  13.3 us (5%)
    pallas_call x1, Pallas kernels, reduce_weights(): pl.pallas_call(lambda *refs: reduce_kernel(factor, *refs), out_shape=(jax...  69.2 us
    all_gather x1, waiting for transfers between devices, body(): normed_all = lax.all_gather(normed, 'mlp', axis=0, tiled=True)  36.2 us
    unnamed x1, blocking collectives  29.7 us
    ppermute x4, starting transfers between devices, passed_along(): lax.ppermute(value, axis, [(i, (i + by) % count) for i in range(count)])  29.5 us
    unnamed x185, local copies, waits for them, and re-layouts  13.7 us
    reduce_sum x1, other arithmetic, body(): centred = mixed - jnp.mean(mixed, axis=-1, keepdims=True)  6.87 us
    ppermute x4, waiting for transfers between devices, passed_along(): lax.ppermute(value, axis, [(i, (i + by) % count) for i in range(count)])  6.77 us
    ppermute x2, starting transfers between devices, with_halo(): lax.ppermute(head, axis, [((i + 1) % count, i) for i in range(ends)])  6.09 us
  transfers between devices with their start and end apart: 11, of which 5 were waited for; matrix products, arithmetic and copies ran while one was open for 11% of the time, Pallas kernels for 27%

profile of v1, /device:TPU:16, one launch (start us, length us, event | category | flops | bytes accessed | tf_op | source)
XLA Modules:
  0.0 260.6 jit_solution(13330175586853975499)
XLA Ops:
  7.2 1.9 reshape.50
  10.2 1.9 collective-permute-start
  12.1 3.6 %collective-permute-start.1 = (bf16[3,23,1024]{2,1,0:T(8,128)(2,1)S(1)}, bf16[3,23,1024]{2,1,0:T(8,128)(2,1)S(1)}, u32[]{:S(2)}, u32[]{:S(2)}) collective-permute-start(bf16[3,23,1024]{2,1,0:T(8,128)(2,1)S(1)} %get-tuple-element.15), channel_id=1, source_target_pairs={{1,0},{2,1},{3,2},{4,3},{5,4},{6,5},{7,6},{9,8},{10,9},{11,10},{12... | collective-permute-start | bytes 423944 | tf_op jit(solution)/shard_map/ppermute | solution.py:229
  18.4 1.2 fusion.113
  19.9 1.7 fusion.114
  21.8 4.3 %collective-permute-start.2 = (bf16[12,3,1024]{2,1,0:T(4,128)(2,1)S(1)}, bf16[12,3,1024]{2,1,0:T(4,128)(2,1)S(1)}, u32[]{:S(2)}, u32[]{:S(2)}) collective-permute-start(bf16[12,3,1024]{2,1,0:T(4,128)(2,1)S(1)} %get-tuple-element.12), channel_id=1, source_target_pairs={{0,8},{8,16},{16,24},{24,32},{32,40},{40,48},{48,56},{56,64},{64,7... | collective-permute-start | bytes 221192 | tf_op jit(solution)/shard_map/ppermute | solution.py:216
  26.7 14.2 %collective-permute-start.3 = (bf16[12,3,1024]{2,1,0:T(4,128)(2,1)S(1)}, bf16[12,3,1024]{2,1,0:T(4,128)(2,1)S(1)}, u32[]{:S(2)}, u32[]{:S(2)}) collective-permute-start(bf16[12,3,1024]{2,1,0:T(4,128)(2,1)S(1)} %get-tuple-element.11), channel_id=1, source_target_pairs={{0,504},{8,0},{16,8},{24,16},{32,24},{40,32},{48,40},{56,48},{64,5... | collective-permute-start | bytes 221192 | tf_op jit(solution)/shard_map/ppermute | solution.py:216
  40.9 4.1 %collective-permute-done.2 = bf16[12,3,1024]{2,1,0:T(4,128)(2,1)S(1)} collective-permute-done((bf16[12,3,1024]{2,1,0:T(4,128)(2,1)S(1)}, bf16[12,3,1024]{2,1,0:T(4,128)(2,1)S(1)}, u32[]{:S(2)}, u32[]{:S(2)}) %collective-permute-start.2) | collective-permute-done | bytes 73760 | tf_op jit(solution)/shard_map/ppermute | solution.py:216
  45.9 1.4 collective-permute-done.3
  47.4 1.3 dynamic_update_slice.6
  49.3 6.9 %fusion.106 = (f32[6,23]{1,0:T(8,128)S(1)}, f32[6,23,1024]{2,1,0:T(8,128)S(1)}) fusion(f32[12,29,1024]{2,1,0:T(8,128)S(1)} %convert_element_type.42, f32[1024]{0:T(1024)} %bitcast.48, f32[1024]{0:T(1024)} %bitcast.47, f32[1024]{0:T(1024)} %bitcast.46, f32[1024]{0:T(1024)} %bitcast.45, f32[1024]{0:T(1024)} %bitcast.44, f32[1024]{0:T(1024)} %bitcast.43, ...), kind=kLoop, calls=%fused_computation.228 | loop fusion | flops 13848438 | bytes 28463656 | tf_op jit(solution)/shard_map/reduce_sum | solution.py:284
  58.1 3.0 %reshape.51 = bf16[1104,1024]{1,0:T(8,128)(2,1)} reshape(bf16[8,138,1024]{2,1,0:T(8,128)(2,1)} %all-gather.5.cloned.1.call-done) | data formatting | bytes 4521984
  61.1 36.2 %all-gather.7.cloned.1.call-done = bf16[8,138,1024]{2,1,0:T(8,128)(2,1)} async-done(((bf16[1,138,1024]{2,1,0:T(8,128)(2,1)}), bf16[8,138,1024]{2,1,0:T(8,128)(2,1)}) %all-gather.7.cloned.1.call-update) | async-done | bytes 2261008 | tf_op jit(solution)/shard_map/all_gather | solution.py:289
  97.3 2.9 %reshape.53 = bf16[1104,1024]{1,0:T(8,128)(2,1)} reshape(bf16[8,138,1024]{2,1,0:T(8,128)(2,1)} %all-gather.7.cloned.1.call-done) | data formatting | bytes 4521984
  100.3 3.1 %fusion.115 = f32[1104,512]{1,0:T(8,128)S(1)} fusion(bf16[1104,1024]{1,0:T(8,128)(2,1)} %reshape.53, bf16[1024,512]{1,0:T(8,128)(2,1)S(1)} %copy-done), kind=kOutput, calls=%fused_computation.236 | convolution fusion | flops 1157627904 | bytes 5570560 | tf_op jit(solution)/shard_map/dot_general | solution.py:291
  103.5 2.0 fusion.1
  106.5 2.7 %convolution_convert_fusion = bf16[1104,1024]{1,0:T(8,128)(2,1)} fusion(bf16[1104,512]{1,0:T(8,128)(2,1)S(1)} %fusion.1, bf16[1024,512]{1,0:T(8,128)(2,1)S(1)} %copy-done), kind=kOutput, calls=%fused_computation | convolution fusion | flops 1158758400 | bytes 4440064 | tf_op jit(solution)/shard_map/dot_general | solution.py:304
  109.3 29.7 %fusion = bf16[144,1024]{1,0:T(8,128)(2,1)S(1)} fusion(bf16[1104,1024]{1,0:T(8,128)(2,1)} %convolution_convert_fusion), kind=kCustom, calls=%all-reduce-scatter | all-reduce-scatter fusion | flops 1179649 | bytes 2557952
  139.0 3.2 %collective-permute-start.8 = (bf16[42,1024]{1,0:T(8,128)(2,1)S(1)}, bf16[42,1024]{1,0:T(8,128)(2,1)S(1)}, u32[]{:S(2)}, u32[]{:S(2)}) collective-permute-start(bf16[42,1024]{1,0:T(8,128)(2,1)S(1)} %slice.812), channel_id=1, source_target_pairs={{0,1},{1,2},{2,3},{3,4},{4,5},{5,6},{6,7},{8,9},{9,10},{10,11},{11... | collective-permute-start | bytes 258056
  142.2 1.3 dynamic-slice.4
  146.4 3.6 %collective-permute-start.4 = (bf16[3,23,1024]{2,1,0:T(8,128)(2,1)S(1)}, bf16[3,23,1024]{2,1,0:T(8,128)(2,1)S(1)}, u32[]{:S(2)}, u32[]{:S(2)}) collective-permute-start(bf16[3,23,1024]{2,1,0:T(8,128)(2,1)S(1)} %get-tuple-element.13), channel_id=1, source_target_pairs={{0,1},{1,2},{2,3},{3,4},{4,5},{5,6},{6,7},{8,9},{9,10},{10,11},{11... | collective-permute-start | bytes 423944 | tf_op jit(solution)/shard_map/ppermute | solution.py:227
  150.0 2.5 collective-permute-start.5
  152.4 3.9 %fusion.6.refs_1_ = f32[512,1024]{1,0:T(8,128)S(1)} fusion(bf16[1104,1024]{1,0:T(8,128)(2,1)} %reshape.51, f32[1104,512]{1,0:T(8,128)} %copy-done.3), kind=kOutput, calls=%fused_computation.10 | convolution fusion | flops 1160454144 | bytes 6619136 | tf_op jit(solution)/shard_map/dot_general | solution.py:297
  156.6 3.5 %collective-permute-start.6 = (bf16[12,3,1024]{2,1,0:T(4,128)(2,1)S(1)}, bf16[12,3,1024]{2,1,0:T(4,128)(2,1)S(1)}, u32[]{:S(2)}, u32[]{:S(2)}) collective-permute-start(bf16[12,3,1024]{2,1,0:T(4,128)(2,1)S(1)} %get-tuple-element.10), channel_id=1, source_target_pairs={{0,8},{8,16},{16,24},{24,32},{32,40},{40,48},{48,56},{56,64},{64,7... | collective-permute-start | bytes 221192 | tf_op jit(solution)/shard_map/ppermute | solution.py:216
  160.1 1.6 fusion.116.refs_0_
  161.7 69.2 %reduce_weights.1 = (bf16[1024,512]{1,0:T(8,128)(2,1)S(1)}, bf16[512,1024]{1,0:T(8,128)(2,1)S(1)}) custom-call(f32[1024,512]{1,0:T(8,128)S(1)} %fusion.116.refs_0_, f32[512,1024]{1,0:T(8,128)S(1)} %fusion.6.refs_1_), custom_call_target="tpu_custom_call" | custom-call | tf_op jit(solution)/shard_map/reduce_weights/pallas_call | solution.py:196
  230.9 7.4 %collective-permute-start.7 = (bf16[12,3,1024]{2,1,0:T(4,128)(2,1)S(1)}, bf16[12,3,1024]{2,1,0:T(4,128)(2,1)S(1)}, u32[]{:S(2)}, u32[]{:S(2)}) collective-permute-start(bf16[12,3,1024]{2,1,0:T(4,128)(2,1)S(1)} %get-tuple-element.9), channel_id=1, source_target_pairs={{0,504},{8,0},{16,8},{24,16},{32,24},{40,32},{48,40},{56,48},{64,5... | collective-permute-start | bytes 221192 | tf_op jit(solution)/shard_map/ppermute | solution.py:216
  238.3 1.9 maximum_maximum_fusion.1
  240.2 1.3 collective-permute-done.7
  241.5 2.7 %dynamic_update_slice.7 = bf16[12,29,1024]{2,1,0:T(8,128)(2,1)} dynamic-update-slice(bf16[12,29,1024]{2,1,0:T(8,128)(2,1)} %maximum_maximum_fusion.1, bf16[12,3,1024]{2,1,0:T(4,128)(2,1)S(1)} %collective-permute-done.7, s32[]{:T(128)} %constant.15.clone.1, s32[]{:T(128)S(6)} %select_n.16, s32[]{:T(128)} %constant.15.clone.1) | dynamic-update-slice | bytes 147460 | tf_op jit(solution)/shard_map/dynamic_update_slice | solution.py:259
  244.5 1.3 convert_element_type.49
  246.2 5.6 %fusion.9 = bf16[6,23,1024]{2,1,0:T(8,128)(2,1)} fusion(f32[12,29,1024]{2,1,0:T(8,128)S(1)} %convert_element_type.49, bf16[6,23,1024]{2,1,0:T(8,128)(2,1)S(1)} %copy-done.5, f32[1024]{0:T(1024)} %bitcast.48, f32[1024]{0:T(1024)} %bitcast.47, f32[1024]{0:T(1024)} %bitcast.46, f32[1024]{0:T(1024)} %bitcast.45, f32[1024]{0:T(1024)} %bitcast.44, ...), kind=kLoop, calls=%fused_computation.16 | loop fusion | flops 14272512 | bytes 28463128 | tf_op jit(solution)/shard_map/convert_element_type | solution.py:332
  (217 shorter events, 13.1 us)
Async XLA Ops:
  7.2 93.1 %copy-start = (bf16[1024,512]{1,0:T(8,128)(2,1)S(1)}, bf16[1024,512]{1,0:T(8,128)(2,1)}, u32[]{:S(2)}) copy-start(bf16[1024,512]{1,0:T(8,128)(2,1)} %param.10) | copy-start | bytes 3145732
  7.2 50.9 %all-gather.5.cloned.1.call-start = ((), (), s32[]{:S(2)}) async-start(), calls=%async_computation | async-start | bytes 2654208 | tf_op jit(solution)/shard_map/all_gather | solution.py:290
  9.1 88.2 %all-gather.7.cloned.1.call-start = ((), (), s32[]{:S(2)}) async-start(), calls=%async_computation.1 | async-start | bytes 2654208 | tf_op jit(solution)/shard_map/all_gather | solution.py:289
  10.2 11.4 %collective-permute-start = (bf16[3,23,1024]{2,1,0:T(8,128)(2,1)S(1)}, bf16[3,23,1024]{2,1,0:T(8,128)(2,1)S(1)}, u32[]{:S(2)}, u32[]{:S(2)}) collective-permute-start(bf16[3,23,1024]{2,1,0:T(8,128)(2,1)S(1)} %get-tuple-element.16), channel_id=1, source_target_pairs={{0,1},{1,2},{2,3},{3,4},{4,5},{5,6},{6,7},{8,9},{9,10},{10,11},{11... | collective-permute-start | bytes 423944 | tf_op jit(solution)/shard_map/ppermute | solution.py:227
  12.1 9.5 %collective-permute-start.1 = (bf16[3,23,1024]{2,1,0:T(8,128)(2,1)S(1)}, bf16[3,23,1024]{2,1,0:T(8,128)(2,1)S(1)}, u32[]{:S(2)}, u32[]{:S(2)}) collective-permute-start(bf16[3,23,1024]{2,1,0:T(8,128)(2,1)S(1)} %get-tuple-element.15), channel_id=1, source_target_pairs={{1,0},{2,1},{3,2},{4,3},{5,4},{6,5},{7,6},{9,8},{10,9},{11,10},{12... | collective-permute-start | bytes 423944 | tf_op jit(solution)/shard_map/ppermute | solution.py:229
  18.3 30.6 %copy-start.6 = (f32[1,1,1024]{2,1,0:T(1,128)}, f32[1,1,1024]{2,1,0:T(1,128)S(1)}, u32[]{:S(2)}) copy-start(f32[1,1,1024]{2,1,0:T(1,128)S(1)} %get-tuple-element.21) | copy-start | bytes 12292
  18.3 30.6 %copy-start.8 = (f32[1,1,1024]{2,1,0:T(1,128)}, f32[1,1,1024]{2,1,0:T(1,128)S(1)}, u32[]{:S(2)}) copy-start(f32[1,1,1024]{2,1,0:T(1,128)S(1)} %get-tuple-element.22) | copy-start | bytes 12292
  18.3 30.6 %copy-start.10 = (f32[1,1,1024]{2,1,0:T(1,128)}, f32[1,1,1024]{2,1,0:T(1,128)S(1)}, u32[]{:S(2)}) copy-start(f32[1,1,1024]{2,1,0:T(1,128)S(1)} %get-tuple-element.23) | copy-start | bytes 12292
  18.3 30.6 %copy-start.12 = (f32[1,1,1024]{2,1,0:T(1,128)}, f32[1,1,1024]{2,1,0:T(1,128)S(1)}, u32[]{:S(2)}) copy-start(f32[1,1,1024]{2,1,0:T(1,128)S(1)} %get-tuple-element.24) | copy-start | bytes 12292
  18.3 30.6 %copy-start.14 = (f32[1,1,1024]{2,1,0:T(1,128)}, f32[1,1,1024]{2,1,0:T(1,128)S(1)}, u32[]{:S(2)}) copy-start(f32[1,1,1024]{2,1,0:T(1,128)S(1)} %get-tuple-element.25) | copy-start | bytes 12292
  18.3 30.6 %copy-start.16 = (f32[1,1,1024]{2,1,0:T(1,128)}, f32[1,1,1024]{2,1,0:T(1,128)S(1)}, u32[]{:S(2)}) copy-start(f32[1,1,1024]{2,1,0:T(1,128)S(1)} %get-tuple-element.26) | copy-start | bytes 12292
  18.3 30.6 %copy-start.18 = (f32[1,1,1024]{2,1,0:T(1,128)}, f32[1,1,1024]{2,1,0:T(1,128)S(1)}, u32[]{:S(2)}) copy-start(f32[1,1,1024]{2,1,0:T(1,128)S(1)} %get-tuple-element.27) | copy-start | bytes 12292
  18.4 30.6 %copy-start.20 = (f32[1,1,1024]{2,1,0:T(1,128)}, f32[1,1,1024]{2,1,0:T(1,128)S(1)}, u32[]{:S(2)}) copy-start(f32[1,1,1024]{2,1,0:T(1,128)S(1)} %get-tuple-element.28) | copy-start | bytes 12292
  18.4 30.6 %copy-start.22 = (f32[1,1,1024]{2,1,0:T(1,128)}, f32[1,1,1024]{2,1,0:T(1,128)S(1)}, u32[]{:S(2)}) copy-start(f32[1,1,1024]{2,1,0:T(1,128)S(1)} %get-tuple-element.29) | copy-start | bytes 12292
  18.4 30.6 %copy-start.24 = (f32[1,1,1024]{2,1,0:T(1,128)}, f32[1,1,1024]{2,1,0:T(1,128)S(1)}, u32[]{:S(2)}) copy-start(f32[1,1,1024]{2,1,0:T(1,128)S(1)} %get-tuple-element.30) | copy-start | bytes 12292
  18.4 30.6 %copy-start.26 = (f32[1,1,1024]{2,1,0:T(1,128)}, f32[1,1,1024]{2,1,0:T(1,128)S(1)}, u32[]{:S(2)}) copy-start(f32[1,1,1024]{2,1,0:T(1,128)S(1)} %get-tuple-element.31) | copy-start | bytes 12292
  18.4 30.6 %copy-start.28 = (f32[1,1,1024]{2,1,0:T(1,128)}, f32[1,1,1024]{2,1,0:T(1,128)S(1)}, u32[]{:S(2)}) copy-start(f32[1,1,1024]{2,1,0:T(1,128)S(1)} %get-tuple-element.32) | copy-start | bytes 12292
  18.4 30.6 %copy-start.30 = (f32[1,1,1024]{2,1,0:T(1,128)}, f32[1,1,1024]{2,1,0:T(1,128)S(1)}, u32[]{:S(2)}) copy-start(f32[1,1,1024]{2,1,0:T(1,128)S(1)} %get-tuple-element.33) | copy-start | bytes 12292
  18.4 30.6 %copy-start.32 = (f32[1,1,1024]{2,1,0:T(1,128)}, f32[1,1,1024]{2,1,0:T(1,128)S(1)}, u32[]{:S(2)}) copy-start(f32[1,1,1024]{2,1,0:T(1,128)S(1)} %get-tuple-element.34) | copy-start | bytes 12292
  18.4 30.6 %copy-start.34 = (f32[1,1,1024]{2,1,0:T(1,128)}, f32[1,1,1024]{2,1,0:T(1,128)S(1)}, u32[]{:S(2)}) copy-start(f32[1,1,1024]{2,1,0:T(1,128)S(1)} %get-tuple-element.35) | copy-start | bytes 12292
  19.7 29.4 %copy-start.36 = (f32[1,1,1024]{2,1,0:T(1,128)}, f32[1,1,1024]{2,1,0:T(1,128)S(1)}, u32[]{:S(2)}) copy-start(f32[1,1,1024]{2,1,0:T(1,128)S(1)} %get-tuple-element.36) | copy-start | bytes 12292
  19.7 29.4 %copy-start.38 = (f32[1,1,1024]{2,1,0:T(1,128)}, f32[1,1,1024]{2,1,0:T(1,128)S(1)}, u32[]{:S(2)}) copy-start(f32[1,1,1024]{2,1,0:T(1,128)S(1)} %get-tuple-element.37) | copy-start | bytes 12292
  19.7 29.4 %copy-start.40 = (f32[1,1,1024]{2,1,0:T(1,128)}, f32[1,1,1024]{2,1,0:T(1,128)S(1)}, u32[]{:S(2)}) copy-start(f32[1,1,1024]{2,1,0:T(1,128)S(1)} %get-tuple-element.38) | copy-start | bytes 12292
  19.7 29.4 %copy-start.42 = (f32[1,1,1024]{2,1,0:T(1,128)}, f32[1,1,1024]{2,1,0:T(1,128)S(1)}, u32[]{:S(2)}) copy-start(f32[1,1,1024]{2,1,0:T(1,128)S(1)} %get-tuple-element.39) | copy-start | bytes 12292
  19.7 29.4 %copy-start.44 = (f32[1,1,1024]{2,1,0:T(1,128)}, f32[1,1,1024]{2,1,0:T(1,128)S(1)}, u32[]{:S(2)}) copy-start(f32[1,1,1024]{2,1,0:T(1,128)S(1)} %get-tuple-element.40) | copy-start | bytes 12292
  21.8 23.2 %collective-permute-start.2 = (bf16[12,3,1024]{2,1,0:T(4,128)(2,1)S(1)}, bf16[12,3,1024]{2,1,0:T(4,128)(2,1)S(1)}, u32[]{:S(2)}, u32[]{:S(2)}) collective-permute-start(bf16[12,3,1024]{2,1,0:T(4,128)(2,1)S(1)} %get-tuple-element.12), channel_id=1, source_target_pairs={{0,8},{8,16},{16,24},{24,32},{32,40},{40,48},{48,56},{56,64},{64,7... | collective-permute-start | bytes 221192 | tf_op jit(solution)/shard_map/ppermute | solution.py:216
  26.7 20.7 %collective-permute-start.3 = (bf16[12,3,1024]{2,1,0:T(4,128)(2,1)S(1)}, bf16[12,3,1024]{2,1,0:T(4,128)(2,1)S(1)}, u32[]{:S(2)}, u32[]{:S(2)}) collective-permute-start(bf16[12,3,1024]{2,1,0:T(4,128)(2,1)S(1)} %get-tuple-element.11), channel_id=1, source_target_pairs={{0,504},{8,0},{16,8},{24,16},{32,24},{40,32},{48,40},{56,48},{64,5... | collective-permute-start | bytes 221192 | tf_op jit(solution)/shard_map/ppermute | solution.py:216
  139.0 5.9 %collective-permute-start.8 = (bf16[42,1024]{1,0:T(8,128)(2,1)S(1)}, bf16[42,1024]{1,0:T(8,128)(2,1)S(1)}, u32[]{:S(2)}, u32[]{:S(2)}) collective-permute-start(bf16[42,1024]{1,0:T(8,128)(2,1)S(1)} %slice.812), channel_id=1, source_target_pairs={{0,1},{1,2},{2,3},{3,4},{4,5},{5,6},{6,7},{8,9},{9,10},{10,11},{11... | collective-permute-start | bytes 258056
  146.4 9.9 %collective-permute-start.4 = (bf16[3,23,1024]{2,1,0:T(8,128)(2,1)S(1)}, bf16[3,23,1024]{2,1,0:T(8,128)(2,1)S(1)}, u32[]{:S(2)}, u32[]{:S(2)}) collective-permute-start(bf16[3,23,1024]{2,1,0:T(8,128)(2,1)S(1)} %get-tuple-element.13), channel_id=1, source_target_pairs={{0,1},{1,2},{2,3},{3,4},{4,5},{5,6},{6,7},{8,9},{9,10},{10,11},{11... | collective-permute-start | bytes 423944 | tf_op jit(solution)/shard_map/ppermute | solution.py:227
  150.0 6.4 %collective-permute-start.5 = (bf16[3,23,1024]{2,1,0:T(8,128)(2,1)S(1)}, bf16[3,23,1024]{2,1,0:T(8,128)(2,1)S(1)}, u32[]{:S(2)}, u32[]{:S(2)}) collective-permute-start(bf16[3,23,1024]{2,1,0:T(8,128)(2,1)S(1)} %get-tuple-element.14), channel_id=1, source_target_pairs={{1,0},{2,1},{3,2},{4,3},{5,4},{6,5},{7,6},{9,8},{10,9},{11,10},{12... | collective-permute-start | bytes 423944 | tf_op jit(solution)/shard_map/ppermute | solution.py:229
  156.6 81.8 %collective-permute-start.6 = (bf16[12,3,1024]{2,1,0:T(4,128)(2,1)S(1)}, bf16[12,3,1024]{2,1,0:T(4,128)(2,1)S(1)}, u32[]{:S(2)}, u32[]{:S(2)}) collective-permute-start(bf16[12,3,1024]{2,1,0:T(4,128)(2,1)S(1)} %get-tuple-element.10), channel_id=1, source_target_pairs={{0,8},{8,16},{16,24},{24,32},{32,40},{40,48},{48,56},{56,64},{64,7... | collective-permute-start | bytes 221192 | tf_op jit(solution)/shard_map/ppermute | solution.py:216
  230.9 10.5 %collective-permute-start.7 = (bf16[12,3,1024]{2,1,0:T(4,128)(2,1)S(1)}, bf16[12,3,1024]{2,1,0:T(4,128)(2,1)S(1)}, u32[]{:S(2)}, u32[]{:S(2)}) collective-permute-start(bf16[12,3,1024]{2,1,0:T(4,128)(2,1)S(1)} %get-tuple-element.9), channel_id=1, source_target_pairs={{0,504},{8,0},{16,8},{24,16},{32,24},{40,32},{48,40},{56,48},{64,5... | collective-permute-start | bytes 221192 | tf_op jit(solution)/shard_map/ppermute | solution.py:216
  (66 other events, 675.1 us)
Sparse Core Ops, SparseCore 0:
  10.7 45.9 all-gather.4
  59.3 37.9 all-gather.6
